TPU v7x, 32 devices: a whole 2x2x4 slice. The times are simulated.
32 devices in a mesh: row: 4 (over y, core), col: 8 (over z, x).
Axes of the slice: x: 2, y: 2, z: 4, core: 2. Of those that a mesh axis runs over, the one named last changes fastest.
Arguments:
- shell_velocity: bfloat16 [256, 128, 128], P(('row', 'col')), may hold values from -6 to 6
- coupling: bfloat16 [256, 2, 2, 256, 128], P(('row', 'col')), may hold values from -0.375 to 0.375
- coupling_dest: int32 [256, 2], P(('row', 'col')), may hold values from 0 to 7, all different within a row; in each aligned block of 8 rows (0 to 7, 8 to 15, ...) at most 2 rows name the same one
- coupling_cluster: int32 [256, 2], P(('row', 'col')), may hold values from 0 to 63
- near_blocks: bfloat16 [4, 8, 32, 2, 256, 256], P('row', 'col'), may hold values from -0.0625 to 0.0625
- far_v: bfloat16 [4, 8, 64, 2, 32, 256], P('row', 'col'), may hold values from -0.25 to 0.25
- far_u: bfloat16 [4, 8, 64, 2, 32, 256], P('row', 'col'), may hold values from -0.125 to 0.125
- block_pairs: int32 [4, 8, 96], P('row', 'col'), may hold values from 0 to 1023, as said below
Outputs:
- response: bfloat16 [16384, 128], P(('row', 'col'))
Inputs may be any that keep to these rules, and one draw needn't show every extreme that they name: `coupling_dest`: the rows of one device name any column group at most 2 times, and some device names one exactly 2 times; the 2 entries of a row differ. `block_pairs`: each entry codes a row cluster r and column cluster c of its group as r * 64 + c; the entries of one group are distinct.
All inputs are finite; a program needn't handle non-finite values.
Results may differ from a plain program's by a relative error of at most 0.008.
Values may be sent and summed in bfloat16 or wider, within the bound.
A program may use at most 128 MiB of HBM per device.

v0:
```python
import jax
import jax.numpy as jnp
from jax import lax
from jax.sharding import PartitionSpec as P

RC_DEV = 16
CC_DEV = 64
NEAR_DEV = 32


def rotate_blocks(values, load_count):
    return jnp.concatenate([-values[..., load_count:], values[..., :load_count]], axis=-1)


def per_device(
    shell_velocity,
    coupling,
    coupling_dest,
    coupling_cluster,
    near_blocks,
    far_v,
    far_u,
    block_pairs,
):
    width = shell_velocity.shape[-1]
    load_count = width // 2
    shell_count = shell_velocity.shape[0]
    top_count = coupling.shape[1]
    panels = coupling.shape[3]
    contributions = jnp.einsum(
        "stpq,sqk->stpk", coupling[:, :, 0], shell_velocity, preferred_element_type=jnp.float32
    )
    contributions = contributions + jnp.einsum(
        "stpq,sqk->stpk",
        coupling[:, :, 1],
        rotate_blocks(shell_velocity, load_count),
        preferred_element_type=jnp.float32,
    )
    entries = shell_count * top_count
    flat_rows = contributions.astype(jnp.bfloat16).reshape(entries, panels * width)
    col_count = lax.axis_size("col")
    capacity = max(2, (entries + col_count - 1) // col_count)
    target = coupling_dest.reshape(entries)
    target_cluster = coupling_cluster.reshape(entries)
    onehot = (target[:, None] == jnp.arange(col_count, dtype=jnp.int32)[None, :]).astype(jnp.int32)
    before = jnp.cumsum(onehot, axis=0) - onehot
    slot_rank = jnp.sum(before * onehot, axis=1)
    slot_index = target * capacity + slot_rank
    slot_pick = jnp.arange(col_count * capacity, dtype=jnp.int32)[:, None] == slot_index[None, :]
    outgoing = jnp.dot(
        slot_pick.astype(jnp.bfloat16), flat_rows, preferred_element_type=jnp.float32
    )
    outgoing = outgoing.astype(jnp.bfloat16).reshape(col_count, capacity, panels, width)
    slot_ids = jnp.sum(slot_pick.astype(jnp.int32) * (target_cluster + 1)[None, :], axis=1) - 1
    slot_ids = slot_ids.reshape(col_count, capacity)
    incoming, got_ids = (
        lax.all_to_all(outgoing, "col", split_axis=0, concat_axis=0, tiled=True),
        lax.all_to_all(slot_ids, "col", split_axis=0, concat_axis=0, tiled=True),
    )
    cluster_pick = (
        jnp.arange(CC_DEV, dtype=jnp.int32)[:, None] == got_ids.reshape(-1)[None, :]
    ).astype(jnp.bfloat16)
    cluster_sums = jnp.dot(
        cluster_pick,
        incoming.reshape(col_count * capacity, panels * width),
        preferred_element_type=jnp.float32,
    ).reshape(CC_DEV, panels, width)
    source_share = lax.psum_scatter(cluster_sums, "row", scatter_dimension=1, tiled=True).astype(
        jnp.bfloat16
    )
    sources = lax.all_gather(source_share, "row", axis=1, tiled=True)
    pair_codes = block_pairs.reshape(-1)
    owners = pair_codes // CC_DEV
    columns = pair_codes % CC_DEV
    nearby_local = near_blocks[0, 0]
    nearby_input = sources[columns[:NEAR_DEV]]
    nearby_contribution = jnp.einsum(
        "dym,dmg->dyg", nearby_local[:, 0], nearby_input, preferred_element_type=jnp.float32
    )
    nearby_contribution = nearby_contribution + jnp.einsum(
        "dym,dmg->dyg",
        nearby_local[:, 1],
        rotate_blocks(nearby_input, load_count),
        preferred_element_type=jnp.float32,
    )
    distant_input = sources[columns[NEAR_DEV:]]
    distant_right_factor = far_v[0, 0]
    expansion_coefficients = jnp.einsum(
        "dyz,dzi->dyi",
        distant_right_factor[:, 0],
        distant_input,
        preferred_element_type=jnp.float32,
    )
    expansion_coefficients = expansion_coefficients + jnp.einsum(
        "dyz,dzi->dyi",
        distant_right_factor[:, 1],
        rotate_blocks(distant_input, load_count),
        preferred_element_type=jnp.float32,
    )
    expansion_coefficients = expansion_coefficients.astype(jnp.bfloat16)
    far_left = far_u[0, 0]
    far_term = jnp.einsum(
        "brp,brk->bpk", far_left[:, 0], expansion_coefficients, preferred_element_type=jnp.float32
    )
    far_term = far_term + jnp.einsum(
        "brp,brk->bpk",
        far_left[:, 1],
        rotate_blocks(expansion_coefficients, load_count),
        preferred_element_type=jnp.float32,
    )
    all_terms = jnp.concatenate([nearby_contribution, far_term], axis=0)
    high_part = all_terms.astype(jnp.bfloat16)
    low_part = (all_terms - high_part.astype(jnp.float32)).astype(jnp.bfloat16)
    owner_pick = (jnp.arange(RC_DEV, dtype=jnp.int32)[:, None] == owners[None, :]).astype(
        jnp.bfloat16
    )
    row_sums = jnp.einsum("ib,bpk->ipk", owner_pick, high_part, preferred_element_type=jnp.float32)
    row_sums = row_sums + jnp.einsum(
        "ib,bpk->ipk", owner_pick, low_part, preferred_element_type=jnp.float32
    )
    row_sums = row_sums.reshape(RC_DEV * panels, width)
    return lax.psum_scatter(row_sums, "col", scatter_dimension=0, tiled=True).astype(jnp.bfloat16)


def solution(mesh):
    return jax.shard_map(
        per_device,
        mesh=mesh,
        in_specs=(
            P(("row", "col"), None, None),
            P(("row", "col"), None, None, None, None),
            P(("row", "col"), None),
            P(("row", "col"), None),
            P("row", "col", None, None, None, None),
            P("row", "col", None, None, None, None),
            P("row", "col", None, None, None, None),
            P("row", "col", None),
        ),
        out_specs=P(("row", "col"), None),
        check_vma=False,
    )
```

profile of v0, /device:TPU:0, one launch (start us, length us, event | category | flops | bytes accessed | tf_op | source)
XLA Modules:
  0.0 330.5 jit_solution(13551763512401435682)
XLA Ops:
  9.5 7.3 %all-to-all-start = ((s32[8,1,2]{2,1,0:T(1,128)}), s32[8,1,2]{2,1,0:T(1,128)S(1)}, u32[]{:S(2)}, u32[]{:S(2)}) async-start(s32[8,1,2]{2,1,0:T(1,128)} %bitcast.2), calls=%async_computation | async-start | bytes 8192 | tf_op jit(solution)/shard_map/all_to_all | solution.py:58
  23.2 5.1 %all-to-all-start.1 = ((bf16[8,2,256,128]{3,2,1,0:T(8,128)(2,1)}), bf16[8,2,256,128]{3,2,1,0:T(8,128)(2,1)S(1)}, u32[]{:S(2)}, u32[]{:S(2)}) async-start(bf16[8,2,256,128]{3,2,1,0:T(8,128)(2,1)} %bitcast.38), calls=%async_computation.1 | async-start | bytes 2097152 | tf_op jit(solution)/shard_map/all_to_all | solution.py:57
  29.6 24.1 %all-to-all-done.1 = bf16[8,2,256,128]{3,2,1,0:T(8,128)(2,1)S(1)} async-done(((bf16[8,2,256,128]{3,2,1,0:T(8,128)(2,1)}), bf16[8,2,256,128]{3,2,1,0:T(8,128)(2,1)S(1)}, u32[]{:S(2)}, u32[]{:S(2)}) %all-to-all-start.1) | async-done | bytes 1048608 | tf_op jit(solution)/shard_map/all_to_all | solution.py:57
  53.7 4.6 %fusion.15 = f32[64,256,128]{2,0,1:T(8,128)} fusion(s32[16]{0:T(128)S(1)} %eq.66, bf16[2,8,256,128]{3,2,1,0:T(8,128)(2,1)S(1)} %bitcast.119), kind=kOutput, calls=%fused_computation.32 | convolution fusion | flops 67109888 | bytes 9437248 | tf_op jit(solution)/shard_map/dot_general | solution.py:63
  58.4 70.3 %reduce-scatter.3.cloned.1.call-done = f32[64,64,128]{2,0,1:T(8,128)} async-done(((f32[64,256,128]{2,0,1:T(8,128)}), f32[64,64,128]{2,0,1:T(8,128)}) %reduce-scatter.3.cloned.1.call-update) | async-done | bytes 2097168 | tf_op jit(solution)/shard_map/reduce_scatter | solution.py:68
  128.7 2.8 convert_element_type.37
  135.6 8.1 %copy.112 = bf16[1,1,32,2,256,256]{5,4,2,3,1,0:T(8,128)(2,1)} copy(bf16[1,1,32,2,256,256]{5,4,3,2,1,0:T(8,128)(2,1)} %param.12) | data formatting | bytes 16777216 | tf_op args[4]
  143.9 22.3 %all-gather.2.cloned.1.call-done = bf16[64,256,128]{2,0,1:T(8,128)(2,1)} async-done(((bf16[64,64,128]{2,0,1:T(8,128)(2,1)}), bf16[64,256,128]{2,0,1:T(8,128)(2,1)}) %all-gather.2.cloned.1.call-update) | async-done | bytes 4194320 | tf_op jit(solution)/shard_map/all_gather | solution.py:71
  166.2 6.8 %copy.73 = bf16[64,256,128]{2,1,0:T(8,128)(2,1)} copy(bf16[64,256,128]{2,0,1:T(8,128)(2,1)} %all-gather.2.cloned.1.call-done) | data formatting | bytes 8388608 | tf_op jit(solution)/shard_map/all_gather | solution.py:71
  173.0 3.1 gather_fusion
  176.1 5.2 %gather_fusion.1 = bf16[64,256,128]{2,1,0:T(8,128)(2,1)} fusion(bf16[64,256,128]{2,1,0:T(8,128)(2,1)} %copy.73, s32[1024]{0:T(1024)S(1)} %pad_clamp_fusion), kind=kCustom, calls=%fused_computation.1 | custom fusion | bytes 8388864 | tf_op jit(solution)/shard_map/gather | solution.py:86
  181.4 2.9 fusion.45
  189.3 4.0 %fusion.1 = f32[32,128,256]{2,1,0:T(8,128)S(1)} fusion(bf16[32,2,256,256]{3,2,0,1:T(8,128)(2,1)} %bitcast.110, bf16[32,256,64]{1,2,0:T(8,128)(2,1)S(1)} %copy.93, bf16[32,256,64]{1,2,0:T(8,128)(2,1)} %neg.13), kind=kOutput, calls=%fused_computation.10 | convolution fusion | flops 541065216 | bytes 10485760 | tf_op jit(solution)/shard_map/dym,dmg->dyg/dot_general | solution.py:80
  193.3 5.8 %add_bitcast_fusion.1 = f32[32,256,128]{1,2,0:T(8,128)} fusion(f32[32,128,256]{2,1,0:T(8,128)S(1)} %fusion.1, bf16[32,256,128]{2,1,0:T(8,128)(2,1)S(1)} %gather_fusion, bf16[32,2,256,256]{3,2,0,1:T(8,128)(2,1)} %bitcast.111), kind=kOutput, calls=%fused_computation.17 | convolution fusion | flops 537919488 | bytes 14680064 | tf_op jit(solution)/shard_map/dym,dmg->dyg/dot_general | solution.py:77
  199.1 2.0 slice_negate_fusion
  201.1 2.3 fusion.3
  206.4 5.0 %add_bitcast_fusion = f32[64,256,128]{1,2,0:T(8,128)} fusion(f32[64,128,256]{2,1,0:T(8,128)S(1)} %fusion.18, bf16[64,2,32,256]{3,2,0,1:T(8,128)(2,1)S(1)} %bitcast.113, bf16[64,32,64]{2,1,0:T(8,128)(2,1)S(1)} %get-tuple-element.10, bf16[64,32,64]{2,1,0:T(8,128)(2,1)S(1)} %get-tuple-element.9), kind=kOutput, calls=%fused_computation.7 | convolution fusion | flops 137363456 | bytes 18874368 | tf_op jit(solution)/shard_map/brp,brk->bpk/dot_general | solution.py:105
  211.4 9.0 %subtract_convert_fusion = bf16[96,256,128]{1,2,0:T(8,128)(2,1)} fusion(f32[64,256,128]{1,2,0:T(8,128)} %add_bitcast_fusion, f32[32,256,128]{1,2,0:T(8,128)} %add_bitcast_fusion.1), kind=kLoop, calls=%fused_computation.4 | loop fusion | flops 15728640 | bytes 18874368 | tf_op jit(solution)/shard_map/convert_element_type | solution.py:113
  220.4 7.9 %fusion = bf16[96,256,128]{1,2,0:T(8,128)(2,1)} fusion(f32[64,256,128]{1,2,0:T(8,128)} %add_bitcast_fusion, f32[32,256,128]{1,2,0:T(8,128)} %add_bitcast_fusion.1), kind=kLoop, calls=%fused_computation.5 | loop fusion | flops 3145728 | bytes 18874368 | tf_op jit(solution)/shard_map/convert_element_type | solution.py:112
  228.3 9.0 %copy.81 = bf16[96,256,128]{2,0,1:T(8,128)(2,1)} copy(bf16[96,256,128]{1,2,0:T(8,128)(2,1)} %fusion) | data formatting | bytes 12582912 | tf_op jit(solution)/shard_map/convert_element_type | solution.py:112
  237.3 9.1 %copy.82 = bf16[96,256,128]{2,0,1:T(8,128)(2,1)} copy(bf16[96,256,128]{1,2,0:T(8,128)(2,1)} %subtract_convert_fusion) | data formatting | bytes 12582912 | tf_op jit(solution)/shard_map/convert_element_type | solution.py:113
  246.4 3.9 %fusion.33 = f32[16,256,128]{2,0,1:T(8,128)S(1)} fusion(bf16[96,256,128]{2,0,1:T(8,128)(2,1)} %copy.81, s32[96]{0:T(128)S(1)} %get-tuple-element.13), kind=kOutput, calls=%fused_computation.61 | convolution fusion | flops 100664832 | bytes 8388992 | tf_op jit(solution)/shard_map/ib,bpk->ipk/dot_general | solution.py:117
  251.9 2.0 copy.83
  253.9 68.5 %reduce-scatter.5.cloned.1.call-done = f32[512,128]{1,0:T(8,128)} async-done(((f32[4096,128]{1,0:T(8,128)}), f32[512,128]{1,0:T(8,128)}) %reduce-scatter.5.cloned.1.call-update) | async-done | bytes 262160 | tf_op jit(solution)/shard_map/reduce_scatter | solution.py:122
  (61 shorter events, 26.0 us)
Async XLA Ops:
  6.5 13.4 %copy-start.4 = (bf16[8,2,2,256,128]{4,3,2,1,0:T(8,128)(2,1)S(1)}, bf16[8,2,2,256,128]{4,3,2,1,0:T(8,128)(2,1)}, u32[]{:S(2)}) copy-start(bf16[8,2,2,256,128]{4,3,2,1,0:T(8,128)(2,1)} %param.9) | copy-start | bytes 6291460
  9.5 13.7 %all-to-all-start = ((s32[8,1,2]{2,1,0:T(1,128)}), s32[8,1,2]{2,1,0:T(1,128)S(1)}, u32[]{:S(2)}, u32[]{:S(2)}) async-start(s32[8,1,2]{2,1,0:T(1,128)} %bitcast.2), calls=%async_computation | async-start | bytes 8192 | tf_op jit(solution)/shard_map/all_to_all | solution.py:58
  23.2 30.5 %all-to-all-start.1 = ((bf16[8,2,256,128]{3,2,1,0:T(8,128)(2,1)}), bf16[8,2,256,128]{3,2,1,0:T(8,128)(2,1)S(1)}, u32[]{:S(2)}, u32[]{:S(2)}) async-start(bf16[8,2,256,128]{3,2,1,0:T(8,128)(2,1)} %bitcast.38), calls=%async_computation.1 | async-start | bytes 2097152 | tf_op jit(solution)/shard_map/all_to_all | solution.py:57
  28.3 100.4 %reduce-scatter.3.cloned.1.call-start = ((), (), s32[]{:S(2)}) async-start(), calls=%async_computation.4 | async-start | bytes 10485760 | tf_op jit(solution)/shard_map/reduce_scatter | solution.py:68
  58.3 73.5 %copy-start.5 = (bf16[1,1,64,2,32,256]{5,4,3,2,1,0:T(8,128)(2,1)S(1)}, bf16[1,1,64,2,32,256]{5,4,3,2,1,0:T(8,128)(2,1)}, u32[]{:S(2)}) copy-start(bf16[1,1,64,2,32,256]{5,4,3,2,1,0:T(8,128)(2,1)} %param.13) | copy-start | bytes 6291460
  58.4 107.8 %all-gather.2.cloned.1.call-start = ((), (), s32[]{:S(2)}) async-start(), calls=%async_computation.5 | async-start | bytes 5242880 | tf_op jit(solution)/shard_map/all_gather | solution.py:71
  131.6 190.8 %reduce-scatter.5.cloned.1.call-start = ((), (), s32[]{:S(2)}) async-start(), calls=%async_computation.6 | async-start | bytes 2359296 | tf_op jit(solution)/shard_map/reduce_scatter | solution.py:122
  131.8 2.4 copy-start.6
  135.6 8.1 %copy-start.7 = (s32[1,1,96]{2,1,0:T(1,128)S(1)}, s32[1,1,96]{2,1,0:T(1,128)}, u32[]{:S(2)}) copy-start(s32[1,1,96]{2,1,0:T(1,128)} %param.15) | copy-start | bytes 1156
  193.3 5.9 %copy-start = (bf16[64,256,128]{2,1,0:T(8,128)(2,1)S(1)}, bf16[64,256,128]{2,1,0:T(8,128)(2,1)}, u32[]{:S(2)}) copy-start(bf16[64,256,128]{2,1,0:T(8,128)(2,1)} %gather_fusion.1) | copy-start | bytes 12582916
  199.1 2.0 copy-start.3
  203.5 1.6 copy-start.2
  246.4 4.6 %copy-start.1 = (bf16[96,256,128]{2,0,1:T(8,128)(2,1)S(1)}, bf16[96,256,128]{2,0,1:T(8,128)(2,1)}, u32[]{:S(2)}) copy-start(bf16[96,256,128]{2,0,1:T(8,128)(2,1)} %copy.82) | copy-start | bytes 18874372
Sparse Core Ops, SparseCore 0:
  58.5 70.2 reduce-scatter.2
  131.7 34.4 all-gather.1
  254.1 68.2 reduce-scatter.4
where the time goes:
time: 332 us; the launch traced here: 331 us
  waiting for transfers between devices  186 us (56%)
  local copies, waits for them, and re-layouts  60.1 us (18%)
  matrix products  31.5 us (9%)
  other arithmetic  26.8 us (8%)
  between operations  13.3 us (4%)
  starting transfers between devices  12.7 us (4%)
    reduce_scatter x1, waiting for transfers between devices, per_device(): lax.psum_scatter(cluster_sums, 'row', scatter_dimension=1, tiled=True)  70.3 us
    reduce_scatter x1, waiting for transfers between devices, per_device(): lax.psum_scatter(row_sums, 'col', scatter_dimension=0, tiled=True)  68.5 us
    all_to_all x1, waiting for transfers between devices, per_device(): lax.all_to_all(outgoing, 'col', split_axis=0, concat_axis=0, tiled=True)  24.1 us
    all_gather x1, waiting for transfers between devices, per_device(): sources = lax.all_gather(source_share, 'row', axis=1, tiled=True)  22.3 us
    unnamed x25, local copies, waits for them, and re-layouts  19.2 us
    convert_element_type x1, local copies, waits for them, and re-layouts, per_device(): low_part = (all_terms - high_part.astype(jnp.float32)).astype(jnp.bfloat16)  9.1 us
    convert_element_type x1, local copies, waits for them, and re-layouts, per_device(): high_part = all_terms.astype(jnp.bfloat16)  9.03 us
    convert_element_type x1, other arithmetic, per_device(): low_part = (all_terms - high_part.astype(jnp.float32)).astype(jnp.bfloat16)  9.01 us
  transfers between devices with their start and end apart: 5, of which 5 were waited for; matrix products, arithmetic and copies ran while one was open for 5% of the time, Pallas kernels for 0%

commit v1 on v0

--- a/solution.py
+++ b/solution.py
@@ -6,6 +6,24 @@
 RC_DEV = 16
 CC_DEV = 64
 NEAR_DEV = 32
+
+
+def laid_out(parts, dim):
+    parts = jnp.moveaxis(parts, 0, dim)
+    shape = parts.shape
+    return parts.reshape(*shape[:dim], shape[dim] * shape[dim + 1], *shape[dim + 2 :])
+
+
+def collected_by_bits(x, axis):
+    size = lax.axis_size(axis)
+    tiles = x[None]
+    for level in range(size.bit_length() - 1):
+        bit = 1 << level
+        received = lax.ppermute(tiles, axis, [(i, i ^ bit) for i in range(size)])
+        both = jnp.stack([tiles, received])
+        upper = lax.axis_index(axis) >> level & 1
+        tiles = jnp.where(upper == 0, both, both[::-1]).reshape(-1, *x.shape)
+    return tiles
 
 
 def rotate_blocks(values, load_count):
@@ -68,7 +86,7 @@
     source_share = lax.psum_scatter(cluster_sums, "row", scatter_dimension=1, tiled=True).astype(
         jnp.bfloat16
     )
-    sources = lax.all_gather(source_share, "row", axis=1, tiled=True)
+    sources = laid_out(collected_by_bits(source_share, "row"), 1)
     pair_codes = block_pairs.reshape(-1)
     owners = pair_codes // CC_DEV
     columns = pair_codes % CC_DEV

time: 332 us -> 351 us (1.057)
  waiting for transfers between devices: 186 us -> 202 us
  other arithmetic: 26.8 us -> 32.3 us
    ppermute x0 -> x2, waiting for transfers between devices: none -> 37.8 us  [collected_by_bits(): received = lax.ppermute(tiles, axis, [(i, i ^ bit) for i in range(size)])]
    all_gather x1 -> x0, waiting for transfers between devices: 22.3 us -> none  [per_device(): sources = lax.all_gather(source_share, 'row', axis=1, tiled=True)]
    another operation x0 -> x4, other arithmetic: none -> 6.9 us  [collected_by_bits(): both = jnp.stack([tiles, received])]
    all_gather x1 -> x0, local copies, waits for them, and re-layouts: 6.82 us -> none  [per_device(): sources = lax.all_gather(source_share, 'row', axis=1, tiled=True)]
    transpose x0 -> x1, local copies, waits for them, and re-layouts: none -> 4.64 us  [laid_out(): parts = jnp.moveaxis(parts, 0, dim)]
    unnamed x25 -> x23, local copies, waits for them, and re-layouts: 19.2 us -> 19.7 us
  transfers between devices with their start and end apart: 5 -> 6, of which waited for: 5 -> 6; matrix products, arithmetic and copies ran while one was open for 5% -> 5% of each run, Pallas kernels for 0% -> 0%
where the time goes in v1:
time: 351 us; the launch traced here: 350 us
  waiting for transfers between devices  202 us (58%)
  local copies, waits for them, and re-layouts  58.3 us (17%)
  other arithmetic  32.3 us (9%)
  matrix products  31.5 us (9%)
  between operations  13.6 us (4%)
  starting transfers between devices  13.1 us (4%)
    reduce_scatter x1, waiting for transfers between devices, per_device(): lax.psum_scatter(cluster_sums, 'row', scatter_dimension=1, tiled=True)  70.1 us
    reduce_scatter x1, waiting for transfers between devices, per_device(): lax.psum_scatter(row_sums, 'col', scatter_dimension=0, tiled=True)  68.6 us
    ppermute x2, waiting for transfers between devices, collected_by_bits(): received = lax.ppermute(tiles, axis, [(i, i ^ bit) for i in range(size)])  37.8 us
    all_to_all x1, waiting for transfers between devices, per_device(): lax.all_to_all(outgoing, 'col', split_axis=0, concat_axis=0, tiled=True)  24.1 us
    unnamed x23, local copies, waits for them, and re-layouts  19.7 us
    convert_element_type x1, local copies, waits for them, and re-layouts, per_device(): low_part = (all_terms - high_part.astype(jnp.float32)).astype(jnp.bfloat16)  9.1 us
    convert_element_type x1, local copies, waits for them, and re-layouts, per_device(): high_part = all_terms.astype(jnp.bfloat16)  9.03 us
    convert_element_type x1, other arithmetic, per_device(): low_part = (all_terms - high_part.astype(jnp.float32)).astype(jnp.bfloat16)  9.01 us
  transfers between devices with their start and end apart: 6, of which 6 were waited for; matrix products, arithmetic and copies ran while one was open for 5% of the time, Pallas kernels for 0%

profile of v1, /device:TPU:0, one launch (start us, length us, event | category | flops | bytes accessed | tf_op | source)
XLA Modules:
  0.0 350.5 jit_solution(88871660595949437)
XLA Ops:
  9.5 7.3 %all-to-all-start = ((s32[8,1,2]{2,1,0:T(1,128)}), s32[8,1,2]{2,1,0:T(1,128)S(1)}, u32[]{:S(2)}, u32[]{:S(2)}) async-start(s32[8,1,2]{2,1,0:T(1,128)} %bitcast.2), calls=%async_computation | async-start | bytes 8192 | tf_op jit(solution)/shard_map/all_to_all | solution.py:76
  23.2 5.1 %all-to-all-start.1 = ((bf16[8,2,256,128]{3,2,1,0:T(8,128)(2,1)}), bf16[8,2,256,128]{3,2,1,0:T(8,128)(2,1)S(1)}, u32[]{:S(2)}, u32[]{:S(2)}) async-start(bf16[8,2,256,128]{3,2,1,0:T(8,128)(2,1)} %bitcast.48), calls=%async_computation.1 | async-start | bytes 2097152 | tf_op jit(solution)/shard_map/all_to_all | solution.py:75
  29.6 24.1 %all-to-all-done.1 = bf16[8,2,256,128]{3,2,1,0:T(8,128)(2,1)S(1)} async-done(((bf16[8,2,256,128]{3,2,1,0:T(8,128)(2,1)}), bf16[8,2,256,128]{3,2,1,0:T(8,128)(2,1)S(1)}, u32[]{:S(2)}, u32[]{:S(2)}) %all-to-all-start.1) | async-done | bytes 1048608 | tf_op jit(solution)/shard_map/all_to_all | solution.py:75
  53.7 4.6 %fusion.17 = f32[64,256,128]{2,0,1:T(8,128)} fusion(s32[16]{0:T(128)S(1)} %eq.74, bf16[2,8,256,128]{3,2,1,0:T(8,128)(2,1)S(1)} %bitcast.136), kind=kOutput, calls=%fused_computation.38 | convolution fusion | flops 67109888 | bytes 9437248 | tf_op jit(solution)/shard_map/dot_general | solution.py:81
  58.6 70.1 %reduce-scatter.3.cloned.1.call-done = f32[64,64,128]{2,0,1:T(8,128)} async-done(((f32[64,256,128]{2,0,1:T(8,128)}), f32[64,64,128]{2,0,1:T(8,128)}) %reduce-scatter.3.cloned.1.call-update) | async-done | bytes 2097168 | tf_op jit(solution)/shard_map/reduce_scatter | solution.py:86
  131.0 2.6 collective-permute-done
  133.8 2.6 fusion.12
  136.7 3.3 copy.107
  141.5 7.6 %copy.105 = bf16[1,1,32,2,256,256]{5,4,2,3,1,0:T(8,128)(2,1)} copy(bf16[1,1,32,2,256,256]{5,4,3,2,1,0:T(8,128)(2,1)} %param.12) | data formatting | bytes 16777216 | tf_op args[4]
  149.2 35.1 %collective-permute-done.1 = bf16[2,64,64,128]{3,1,2,0:T(8,128)(2,1)} collective-permute-done((bf16[2,64,64,128]{3,1,2,0:T(8,128)(2,1)}, bf16[2,64,64,128]{3,1,2,0:T(8,128)(2,1)}, u32[]{:S(2)}, u32[]{:S(2)}) %collective-permute-start.1) | collective-permute-done | bytes 2097184 | tf_op jit(solution)/shard_map/ppermute | solution.py:22
  188.0 4.6 %copy.67 = bf16[64,4,64,128]{3,2,1,0:T(8,128)(2,1)} copy(bf16[64,4,64,128]{3,0,2,1:T(8,128)(2,1)S(1)} %bitcast.128) | data formatting | bytes 8388608 | tf_op jit(solution)/shard_map/transpose | solution.py:12
  192.7 3.1 gather_fusion
  195.8 5.2 %gather_fusion.1 = bf16[64,256,128]{2,1,0:T(8,128)(2,1)} fusion(bf16[64,256,128]{2,1,0:T(8,128)(2,1)} %bitcast.127, s32[1024]{0:T(1024)S(1)} %pad_clamp_fusion), kind=kCustom, calls=%fused_computation.1 | custom fusion | bytes 8388864 | tf_op jit(solution)/shard_map/gather | solution.py:104
  201.1 2.9 fusion.47
  208.9 4.0 %fusion.1 = f32[32,128,256]{2,1,0:T(8,128)S(1)} fusion(bf16[32,2,256,256]{3,2,0,1:T(8,128)(2,1)} %bitcast.124, bf16[32,256,64]{1,2,0:T(8,128)(2,1)S(1)} %copy.86, bf16[32,256,64]{1,2,0:T(8,128)(2,1)} %neg.13), kind=kOutput, calls=%fused_computation.11 | convolution fusion | flops 541065216 | bytes 10485760 | tf_op jit(solution)/shard_map/dym,dmg->dyg/dot_general | solution.py:98
  213.0 5.8 %add_bitcast_fusion.1 = f32[32,256,128]{1,2,0:T(8,128)} fusion(f32[32,128,256]{2,1,0:T(8,128)S(1)} %fusion.1, bf16[32,256,128]{2,1,0:T(8,128)(2,1)S(1)} %gather_fusion, bf16[32,2,256,256]{3,2,0,1:T(8,128)(2,1)} %bitcast.125), kind=kOutput, calls=%fused_computation.19 | convolution fusion | flops 537919488 | bytes 14680064 | tf_op jit(solution)/shard_map/dym,dmg->dyg/dot_general | solution.py:95
  220.6 2.3 fusion.3
  225.8 5.0 %add_bitcast_fusion = f32[64,256,128]{1,2,0:T(8,128)} fusion(f32[64,128,256]{2,1,0:T(8,128)S(1)} %fusion.20, bf16[64,2,32,256]{3,2,0,1:T(8,128)(2,1)S(1)} %bitcast.130, bf16[64,32,64]{2,1,0:T(8,128)(2,1)S(1)} %get-tuple-element.14, bf16[64,32,64]{2,1,0:T(8,128)(2,1)S(1)} %get-tuple-element.13), kind=kOutput, calls=%fused_computation.7 | convolution fusion | flops 137363456 | bytes 18874368 | tf_op jit(solution)/shard_map/brp,brk->bpk/dot_general | solution.py:123
  230.9 9.0 %subtract_convert_fusion = bf16[96,256,128]{1,2,0:T(8,128)(2,1)} fusion(f32[64,256,128]{1,2,0:T(8,128)} %add_bitcast_fusion, f32[32,256,128]{1,2,0:T(8,128)} %add_bitcast_fusion.1), kind=kLoop, calls=%fused_computation.4 | loop fusion | flops 15728640 | bytes 18874368 | tf_op jit(solution)/shard_map/convert_element_type | solution.py:131
  239.9 7.9 %fusion = bf16[96,256,128]{1,2,0:T(8,128)(2,1)} fusion(f32[64,256,128]{1,2,0:T(8,128)} %add_bitcast_fusion, f32[32,256,128]{1,2,0:T(8,128)} %add_bitcast_fusion.1), kind=kLoop, calls=%fused_computation.5 | loop fusion | flops 3145728 | bytes 18874368 | tf_op jit(solution)/shard_map/convert_element_type | solution.py:130
  247.7 9.0 %copy.74 = bf16[96,256,128]{2,0,1:T(8,128)(2,1)} copy(bf16[96,256,128]{1,2,0:T(8,128)(2,1)} %fusion) | data formatting | bytes 12582912 | tf_op jit(solution)/shard_map/convert_element_type | solution.py:130
  256.7 9.1 %copy.75 = bf16[96,256,128]{2,0,1:T(8,128)(2,1)} copy(bf16[96,256,128]{1,2,0:T(8,128)(2,1)} %subtract_convert_fusion) | data formatting | bytes 12582912 | tf_op jit(solution)/shard_map/convert_element_type | solution.py:131
  265.9 3.9 %fusion.35 = f32[16,256,128]{2,0,1:T(8,128)S(1)} fusion(bf16[96,256,128]{2,0,1:T(8,128)(2,1)} %copy.74, s32[96]{0:T(128)S(1)} %get-tuple-element.17), kind=kOutput, calls=%fused_computation.69 | convolution fusion | flops 100664832 | bytes 8388992 | tf_op jit(solution)/shard_map/ib,bpk->ipk/dot_general | solution.py:135
  273.4 68.6 %reduce-scatter.5.cloned.1.call-done = f32[512,128]{1,0:T(8,128)} async-done(((f32[4096,128]{1,0:T(8,128)}), f32[512,128]{1,0:T(8,128)}) %reduce-scatter.5.cloned.1.call-update) | async-done | bytes 262160 | tf_op jit(solution)/shard_map/reduce_scatter | solution.py:140
  (64 shorter events, 33.8 us)
Async XLA Ops:
  6.5 13.4 %copy-start.4 = (bf16[8,2,2,256,128]{4,3,2,1,0:T(8,128)(2,1)S(1)}, bf16[8,2,2,256,128]{4,3,2,1,0:T(8,128)(2,1)}, u32[]{:S(2)}) copy-start(bf16[8,2,2,256,128]{4,3,2,1,0:T(8,128)(2,1)} %param.9) | copy-start | bytes 6291460
  9.5 13.7 %all-to-all-start = ((s32[8,1,2]{2,1,0:T(1,128)}), s32[8,1,2]{2,1,0:T(1,128)S(1)}, u32[]{:S(2)}, u32[]{:S(2)}) async-start(s32[8,1,2]{2,1,0:T(1,128)} %bitcast.2), calls=%async_computation | async-start | bytes 8192 | tf_op jit(solution)/shard_map/all_to_all | solution.py:76
  23.2 30.5 %all-to-all-start.1 = ((bf16[8,2,256,128]{3,2,1,0:T(8,128)(2,1)}), bf16[8,2,256,128]{3,2,1,0:T(8,128)(2,1)S(1)}, u32[]{:S(2)}, u32[]{:S(2)}) async-start(bf16[8,2,256,128]{3,2,1,0:T(8,128)(2,1)} %bitcast.48), calls=%async_computation.1 | async-start | bytes 2097152 | tf_op jit(solution)/shard_map/all_to_all | solution.py:75
  28.3 100.4 %reduce-scatter.3.cloned.1.call-start = ((), (), s32[]{:S(2)}) async-start(), calls=%async_computation.4 | async-start | bytes 10485760 | tf_op jit(solution)/shard_map/reduce_scatter | solution.py:86
  58.3 283.7 %reduce-scatter.5.cloned.1.call-start = ((), (), s32[]{:S(2)}) async-start(), calls=%async_computation.5 | async-start | bytes 2359296 | tf_op jit(solution)/shard_map/reduce_scatter | solution.py:140
  130.9 2.7 collective-permute-start
  136.4 48.0 %collective-permute-start.1 = (bf16[2,64,64,128]{3,1,2,0:T(8,128)(2,1)}, bf16[2,64,64,128]{3,1,2,0:T(8,128)(2,1)}, u32[]{:S(2)}, u32[]{:S(2)}) collective-permute-start(bf16[2,64,64,128]{3,1,2,0:T(8,128)(2,1)} %get-tuple-element.10), channel_id=1, source_target_pairs={{0,16},{8,24},{16,0},{24,8},{1,17},{9,25},{17,1},{25,9},{2,18},{10... | collective-permute-start | bytes 6291464 | tf_op jit(solution)/shard_map/ppermute | solution.py:22
  136.7 3.3 copy-start.5
  141.5 7.6 %copy-start.6 = (s32[1,1,96]{2,1,0:T(1,128)S(1)}, s32[1,1,96]{2,1,0:T(1,128)}, u32[]{:S(2)}) copy-start(s32[1,1,96]{2,1,0:T(1,128)} %param.15) | copy-start | bytes 1156
  213.0 5.8 %copy-start = (bf16[64,256,128]{2,1,0:T(8,128)(2,1)S(1)}, bf16[64,256,128]{2,1,0:T(8,128)(2,1)}, u32[]{:S(2)}) copy-start(bf16[64,256,128]{2,1,0:T(8,128)(2,1)} %gather_fusion.1) | copy-start | bytes 12582916
  218.8 1.8 copy-start.3
  222.9 1.6 copy-start.2
  265.9 4.6 %copy-start.1 = (bf16[96,256,128]{2,0,1:T(8,128)(2,1)S(1)}, bf16[96,256,128]{2,0,1:T(8,128)(2,1)}, u32[]{:S(2)}) copy-start(bf16[96,256,128]{2,0,1:T(8,128)(2,1)} %copy.75) | copy-start | bytes 18874372
Sparse Core Ops, SparseCore 0:
  58.5 70.2 reduce-scatter.2
  273.5 68.4 reduce-scatter.4
